TPU v7x, 32 devices: a whole 2x2x4 slice. The times are simulated.
32 devices in a mesh: seq: 4 (over x, core), batch: 8 (over z, y).
Axes of the slice: x: 2, y: 2, z: 4, core: 2. Of those that a mesh axis runs over, the one named last changes fastest.
Arguments:
- tokens: bfloat16 [8, 1024, 1024], P('batch', 'seq'), may hold values from -6 to 6
- w_query: bfloat16 [1024, 1024], P(('seq', 'batch')), may hold values from -0.25 to 0.25
- w_key: bfloat16 [1024, 1024], P(('seq', 'batch')), may hold values from -0.25 to 0.25
- w_value: bfloat16 [1024, 1024], P(('seq', 'batch')), may hold values from -0.1875 to 0.1875
- w_out: bfloat16 [1024, 1024], P(('seq', 'batch')), may hold values from -0.375 to 0.375
- gain_attn: bfloat16 [1024], P(('seq', 'batch')), may hold values from 0.25 to 1.75
- w_gate: bfloat16 [1024, 4096], P(('seq', 'batch')), may hold values from -0.1875 to 0.1875
- w_up: bfloat16 [1024, 4096], P(('seq', 'batch')), may hold values from -0.1875 to 0.1875
- w_down: bfloat16 [4096, 1024], P(('seq', 'batch')), may hold values from -0.125 to 0.125
- gain_ffn: bfloat16 [1024], P(('seq', 'batch')), may hold values from 0.25 to 1.75
- counts: int32 [8, 4], P('batch'), may hold values from 0 to 256, as said below
- cotangent: bfloat16 [8, 1024, 1024], P('batch', 'seq'), may hold values from -6 to 6
Outputs:
- block_output: bfloat16 [8, 1024, 1024], P('batch', 'seq')
- input_grad: float32 [8, 1024, 1024], P('batch', 'seq')
- grad_w_query: float32 [1024, 1024], P(('seq', 'batch'))
- grad_w_key: float32 [1024, 1024], P(('seq', 'batch'))
- grad_w_value: float32 [1024, 1024], P(('seq', 'batch'))
- grad_w_out: float32 [1024, 1024], P(('seq', 'batch'))
- grad_gain_attn: float32 [1024], P(('seq', 'batch'))
- grad_w_gate: float32 [1024, 4096], P(('seq', 'batch'))
- grad_w_up: float32 [1024, 4096], P(('seq', 'batch'))
- grad_w_down: float32 [4096, 1024], P(('seq', 'batch'))
- grad_gain_ffn: float32 [1024], P(('seq', 'batch'))
Inputs may be any that keep to these rules, and one draw needn't show every extreme that they name: counts[s, i] = min(max(L_s - i * 256, 0), 256) for a length L_s of sequence s between 256 and 1024; some sequence has length 1024 and another length 256.
All inputs are finite; a program needn't handle non-finite values.
Results may differ from a plain program's by a relative error of at most 0.017.
Values may be sent and summed in bfloat16 or wider, within the bound.
No kernel may reach another device: no remote copies, remote signals or barrier semaphores. Data moves between devices by JAX's collectives and lax.ppermute only.
A program may use at most 192 MiB of HBM per device.

v0:
```python
import math
import jax
import jax.numpy as jnp
from jax import lax
from jax.sharding import PartitionSpec as P

HEADS = 16
EPSILON = 1e-05


def rms_scale(source):
    return lax.rsqrt(jnp.mean(source * source, axis=-1, keepdims=True) + EPSILON)


def norm_back(incoming, source, gain_full):
    inverse = rms_scale(source)
    scaled = incoming * gain_full
    grad_source = inverse * (
        scaled - source * (inverse * inverse) * jnp.mean(scaled * source, axis=-1, keepdims=True)
    )
    grad_gain = jnp.sum(incoming * source * inverse, axis=0)
    return (grad_source, grad_gain)


def project(left, right):
    return jnp.dot(left, right, preferred_element_type=jnp.float32)


def project_back(grad_rows, weight):
    return jnp.einsum("td,ed->te", grad_rows, weight, preferred_element_type=jnp.float32)


def weight_grad(left, grad_rows):
    return jnp.einsum("td,te->de", left, grad_rows, preferred_element_type=jnp.float32)


def column_grad(left, grad_rows):
    return weight_grad(left, grad_rows)


def local(
    tokens,
    w_query,
    w_key,
    w_value,
    w_out,
    gain_attn,
    w_gate,
    w_up,
    w_down,
    gain_ffn,
    counts,
    cotangent,
):
    source = tokens[0].astype(jnp.float32)
    row_count, model_width = source.shape
    head_count = HEADS
    head_width = model_width // head_count
    shard_count = lax.axis_size("seq")
    shard_index = lax.axis_index("seq")
    seq_length = row_count * shard_count
    score_scale = head_width ** (-0.5)
    score_offset = -math.log(seq_length)
    count_row = counts[0]
    query_first = shard_index * row_count
    query_last = query_first + row_count - 1
    query_pos = query_first + jnp.arange(row_count, dtype=jnp.int32)
    shard_ids = jnp.arange(shard_count, dtype=jnp.int32)

    def split_heads(matrix):
        return matrix.reshape(matrix.shape[0], head_count, head_width)

    def gating(query_heads, key_block):
        key_rows = key_block.shape[0]
        logits = (
            jnp.einsum(
                "qhe,khe->hqk",
                query_heads,
                split_heads(key_block),
                preferred_element_type=jnp.float32,
            )
            * score_scale
            + score_offset
        )
        key_pos = jnp.arange(key_rows, dtype=jnp.int32)
        owner = key_pos // row_count
        place = key_pos - owner * row_count
        valid_count = jnp.sum(
            jnp.where(owner[:, None] == shard_ids[None, :], count_row[None, :], 0), axis=1
        )
        allowed = (place < valid_count)[None, :] & (key_pos[None, :] <= query_pos[:, None])
        return (jax.nn.sigmoid(logits), allowed[None])

    def unchanged(carry):
        return carry

    attn_full = (
        lax.all_gather(w_query, ("seq", "batch"), axis=0, tiled=True),
        lax.all_gather(w_key, ("seq", "batch"), axis=0, tiled=True),
        lax.all_gather(w_value, ("seq", "batch"), axis=0, tiled=True),
        lax.all_gather(w_out, ("seq", "batch"), axis=0, tiled=True),
        lax.all_gather(gain_attn, ("seq", "batch"), axis=0, tiled=True),
    )
    gain_one = attn_full[4].astype(jnp.float32)
    normed_attn = (source * rms_scale(source) * gain_one).astype(jnp.bfloat16)
    query = project(normed_attn, attn_full[0]).astype(jnp.bfloat16)
    key_rows_mine = project(normed_attn, attn_full[1]).astype(jnp.bfloat16)
    value_rows_mine = project(normed_attn, attn_full[2]).astype(jnp.bfloat16)
    query_heads = split_heads(query)
    key_block = lax.all_gather(key_rows_mine, "seq", axis=0, tiled=True)
    value_block = lax.all_gather(value_rows_mine, "seq", axis=0, tiled=True)

    def attend_compute(summed):
        gates, allowed = gating(query_heads, key_block)
        probs = jnp.where(allowed, gates, 0.0).astype(jnp.bfloat16)
        mixed = jnp.einsum(
            "hqk,khe->qhe", probs, split_heads(value_block), preferred_element_type=jnp.float32
        )
        return mixed.reshape(row_count, model_width)

    attended_sum = lax.cond(
        jnp.int32(0) <= query_last,
        attend_compute,
        unchanged,
        jnp.zeros((row_count, model_width), jnp.float32),
    )
    attended = attended_sum.astype(jnp.bfloat16)
    resid = source + project(attended, attn_full[3])
    ffn_full = (
        lax.all_gather(w_gate, ("seq", "batch"), axis=0, tiled=True),
        lax.all_gather(w_up, ("seq", "batch"), axis=0, tiled=True),
        lax.all_gather(w_down, ("seq", "batch"), axis=0, tiled=True),
        lax.all_gather(gain_ffn, ("seq", "batch"), axis=0, tiled=True),
    )
    gain_two = ffn_full[3].astype(jnp.float32)
    normed_ffn = (resid * rms_scale(resid) * gain_two).astype(jnp.bfloat16)
    gate = project(normed_ffn, ffn_full[0])
    up_proj = project(normed_ffn, ffn_full[1])
    gate_sigma = jax.nn.sigmoid(gate)
    hidden = (gate * gate_sigma * up_proj).astype(jnp.bfloat16)
    block_output = (resid + project(hidden, ffn_full[2])).astype(jnp.bfloat16)
    ffn_back = (
        lax.all_gather(w_gate, ("seq", "batch"), axis=0, tiled=True),
        lax.all_gather(w_up, ("seq", "batch"), axis=0, tiled=True),
        lax.all_gather(w_down, ("seq", "batch"), axis=0, tiled=True),
        lax.all_gather(gain_ffn, ("seq", "batch"), axis=0, tiled=True),
    )
    cot_rows = cotangent[0]
    grad_hidden = project_back(cot_rows, ffn_back[2])
    grad_gate = (
        grad_hidden * up_proj * (gate_sigma + gate * gate_sigma * (1.0 - gate_sigma))
    ).astype(jnp.bfloat16)
    grad_up = (grad_hidden * gate * gate_sigma).astype(jnp.bfloat16)
    grad_normed_ffn = project_back(grad_gate, ffn_back[0]) + project_back(grad_up, ffn_back[1])
    grad_norm_two, grad_gain_ffn = norm_back(grad_normed_ffn, resid, gain_two)
    grad_resid = cot_rows.astype(jnp.float32) + grad_norm_two
    grad_w_gate = lax.psum_scatter(
        column_grad(normed_ffn, grad_gate), ("seq", "batch"), scatter_dimension=0, tiled=True
    )
    grad_w_up = lax.psum_scatter(
        column_grad(normed_ffn, grad_up), ("seq", "batch"), scatter_dimension=0, tiled=True
    )
    grad_w_down = lax.psum_scatter(
        column_grad(hidden, cot_rows), ("seq", "batch"), scatter_dimension=0, tiled=True
    )
    attn_back = (
        lax.all_gather(w_query, ("seq", "batch"), axis=0, tiled=True),
        lax.all_gather(w_key, ("seq", "batch"), axis=0, tiled=True),
        lax.all_gather(w_value, ("seq", "batch"), axis=0, tiled=True),
        lax.all_gather(w_out, ("seq", "batch"), axis=0, tiled=True),
        lax.all_gather(gain_attn, ("seq", "batch"), axis=0, tiled=True),
    )
    resid_low = grad_resid.astype(jnp.bfloat16)
    grad_attended = project_back(resid_low, attn_back[3]).astype(jnp.bfloat16)
    grad_heads = split_heads(grad_attended)
    start_state = (
        jnp.zeros((row_count, model_width), jnp.float32),
        jnp.zeros((seq_length, model_width), jnp.float32),
        jnp.zeros((seq_length, model_width), jnp.float32),
    )
    reverse_key_block = lax.all_gather(key_rows_mine, "seq", axis=0, tiled=True)
    reverse_value_block = lax.all_gather(value_rows_mine, "seq", axis=0, tiled=True)

    def reverse_compute(summed):
        key_rows = reverse_key_block.shape[0]
        key_heads = split_heads(reverse_key_block)
        gates, allowed = gating(query_heads, reverse_key_block)
        probs = jnp.where(allowed, gates, 0.0).astype(jnp.bfloat16)
        value_term = jnp.einsum(
            "hqk,qhe->khe", probs, grad_heads, preferred_element_type=jnp.float32
        ).reshape(key_rows, model_width)
        grad_probs = jnp.einsum(
            "qhe,khe->hqk",
            grad_heads,
            split_heads(reverse_value_block),
            preferred_element_type=jnp.float32,
        )
        grad_scores = jnp.where(allowed, grad_probs * gates * (1.0 - gates), 0.0).astype(
            jnp.bfloat16
        )
        query_term = (
            jnp.einsum("hqk,khe->qhe", grad_scores, key_heads, preferred_element_type=jnp.float32)
            * score_scale
        )
        key_term = (
            jnp.einsum("hqk,qhe->khe", grad_scores, query_heads, preferred_element_type=jnp.float32)
            * score_scale
        ).reshape(key_rows, model_width)
        grad_query_sum = query_term.reshape(row_count, model_width)
        return (grad_query_sum, key_term, value_term)

    grad_query_sum, grad_key_full, grad_value_full = lax.cond(
        jnp.int32(0) <= query_last, reverse_compute, unchanged, start_state
    )
    grad_key_mine, grad_value_mine = (
        lax.psum_scatter(
            grad_key_full.astype(jnp.bfloat16), "seq", scatter_dimension=0, tiled=True
        ).astype(jnp.float32),
        lax.psum_scatter(
            grad_value_full.astype(jnp.bfloat16), "seq", scatter_dimension=0, tiled=True
        ).astype(jnp.float32),
    )
    grad_query = grad_query_sum.astype(jnp.bfloat16)
    grad_key = grad_key_mine.astype(jnp.bfloat16)
    grad_value = grad_value_mine.astype(jnp.bfloat16)
    grad_normed_attn = (
        project_back(grad_query, attn_back[0])
        + project_back(grad_key, attn_back[1])
        + project_back(grad_value, attn_back[2])
    )
    grad_norm_one, grad_gain_attn = norm_back(grad_normed_attn, source, gain_one)
    input_grad = grad_resid + grad_norm_one
    projected_grads = jnp.concatenate([grad_query, grad_key, grad_value], axis=1)
    attn_grads = lax.psum_scatter(
        jnp.concatenate(
            [column_grad(normed_attn, projected_grads), column_grad(attended, resid_low)], axis=1
        ),
        ("seq", "batch"),
        scatter_dimension=0,
        tiled=True,
    )
    gain_attn_mine, gain_ffn_mine = (
        lax.psum_scatter(grad_gain_attn, ("seq", "batch"), scatter_dimension=0, tiled=True),
        lax.psum_scatter(grad_gain_ffn, ("seq", "batch"), scatter_dimension=0, tiled=True),
    )
    grad_w_query = attn_grads[:, :model_width]
    grad_w_key = attn_grads[:, model_width : 2 * model_width]
    grad_w_value = attn_grads[:, 2 * model_width : 3 * model_width]
    grad_w_out = attn_grads[:, 3 * model_width :]
    return (
        block_output[None],
        input_grad[None],
        grad_w_query,
        grad_w_key,
        grad_w_value,
        grad_w_out,
        gain_attn_mine,
        grad_w_gate,
        grad_w_up,
        grad_w_down,
        gain_ffn_mine,
    )


def solution(mesh):
    in_specs = (
        P("batch", "seq", None),
        P(("seq", "batch"), None),
        P(("seq", "batch"), None),
        P(("seq", "batch"), None),
        P(("seq", "batch"), None),
        P(("seq", "batch")),
        P(("seq", "batch"), None),
        P(("seq", "batch"), None),
        P(("seq", "batch"), None),
        P(("seq", "batch")),
        P("batch", None),
        P("batch", "seq", None),
    )
    out_specs = (
        P("batch", "seq", None),
        P("batch", "seq", None),
        P(("seq", "batch"), None),
        P(("seq", "batch"), None),
        P(("seq", "batch"), None),
        P(("seq", "batch"), None),
        P(("seq", "batch")),
        P(("seq", "batch"), None),
        P(("seq", "batch"), None),
        P(("seq", "batch"), None),
        P(("seq", "batch")),
    )
    return jax.shard_map(local, mesh=mesh, in_specs=in_specs, out_specs=out_specs, check_vma=False)
```

profile of v0, /device:TPU:0, one launch (start us, length us, event | category | flops | bytes accessed | tf_op | source)
XLA Modules:
  0.0 2127.6 jit_solution(17704540515414183479)
XLA Ops:
  11.2 42.1 %all-reduce.5 = (bf16[1024]{0:T(1024)(128)(2,1)S(1)}, bf16[1024]{0:T(1024)(128)(2,1)S(1)}) all-reduce(bf16[1024]{0:T(1024)(128)(2,1)S(1)} %dynamic-update-slice, bf16[1024]{0:T(1024)(128)(2,1)S(1)} %dynamic-update-slice.1), channel_id=1, replica_groups=mesh['seq'=4,'batch'=8] {'seq','batch'}, use_global_device_ids=true, to_apply=%add | all-reduce | flops 2048 | bytes 8192
  55.0 15.1 all-gather.10.cloned.1.call-done
  73.5 54.8 %all-gather.16.cloned.1.call-done = bf16[1024,1024]{1,0:T(8,128)(2,1)} async-done(((bf16[32,1024]{1,0:T(8,128)(2,1)}), bf16[1024,1024]{1,0:T(8,128)(2,1)}) %all-gather.16.cloned.1.call-update) | async-done | bytes 2097168 | tf_op jit(solution)/shard_map/all_gather | solution.py:100
  134.4 52.2 %all-gather.14.cloned.1.call-done = bf16[1024,1024]{1,0:T(8,128)(2,1)} async-done(((bf16[32,1024]{1,0:T(8,128)(2,1)}), bf16[1024,1024]{1,0:T(8,128)(2,1)}) %all-gather.14.cloned.1.call-update) | async-done | bytes 2097168 | tf_op jit(solution)/shard_map/all_gather | solution.py:98
  189.9 20.1 all-gather.12.cloned.1.call-done
  210.0 24.6 %all-gather.18.cloned.1.call-done = bf16[1024,1024]{1,0:T(8,128)(2,1)} async-done(((bf16[256,1024]{1,0:T(8,128)(2,1)}), bf16[1024,1024]{1,0:T(8,128)(2,1)}) %all-gather.18.cloned.1.call-update) | async-done | bytes 2097168 | tf_op jit(solution)/shard_map/all_gather | solution.py:111
  234.6 16.6 conditional.2
  251.2 42.6 %all-gather.20.cloned.1.call-done = bf16[1024,1024]{1,0:T(8,128)(2,1)} async-done(((bf16[32,1024]{1,0:T(8,128)(2,1)}), bf16[1024,1024]{1,0:T(8,128)(2,1)}) %all-gather.20.cloned.1.call-update) | async-done | bytes 2097168 | tf_op jit(solution)/shard_map/all_gather | solution.py:101
  296.4 76.3 %all-gather.22.cloned.1.call-done = bf16[1024,4096]{1,0:T(8,128)(2,1)} async-done(((bf16[32,4096]{1,0:T(8,128)(2,1)}), bf16[1024,4096]{1,0:T(8,128)(2,1)}) %all-gather.22.cloned.1.call-update) | async-done | bytes 8388624 | tf_op jit(solution)/shard_map/all_gather | solution.py:130
  380.4 71.0 %all-gather.24.cloned.1.call-done = bf16[1024,4096]{1,0:T(8,128)(2,1)} async-done(((bf16[32,4096]{1,0:T(8,128)(2,1)}), bf16[1024,4096]{1,0:T(8,128)(2,1)}) %all-gather.24.cloned.1.call-update) | async-done | bytes 8388624 | tf_op jit(solution)/shard_map/all_gather | solution.py:131
  459.2 71.0 %all-gather.26.cloned.1.call-done = bf16[4096,1024]{1,0:T(8,128)(2,1)} async-done(((bf16[128,1024]{1,0:T(8,128)(2,1)}), bf16[4096,1024]{1,0:T(8,128)(2,1)}) %all-gather.26.cloned.1.call-update) | async-done | bytes 8388624 | tf_op jit(solution)/shard_map/all_gather | solution.py:132
  530.2 12.5 multiply_convert_fusion
  554.6 52.7 %conditional.3 = (bf16[1024,1024]{0,1:T(8,128)(2,1)}, bf16[1024,1024]{0,1:T(8,128)(2,1)}, bf16[256,1024]{0,1:T(8,128)(2,1)}) conditional(s32[]{:T(128)} %convert_element_type.97, () %tuple.28, (s32[4]{0:T(128)S(1)}, s32[1,4]{1,0:T(1,128)S(1)}, s32[256]{0:T(256)S(1)}, bf16[256,1024]{1,0:T(8,128)(2,1)}, bf16[1024,1024]{1,0:T(8,128)(2,1)}, ...), branch_computations={%region_6.7_spmd, %region_7.9_spmd} | conditional | flops 2733668352 | bytes 136596672 | solution.py:212
  574.9 13.4 select_convert_fusion.2
  611.8 25.4 %reduce-scatter.7.cloned.1.call-done = bf16[256,1024]{0,1:T(8,128)(2,1)} async-done(((bf16[1024,1024]{0,1:T(8,128)(2,1)}), bf16[256,1024]{0,1:T(8,128)(2,1)}) %reduce-scatter.7.cloned.1.call-update) | async-done | bytes 524304 | tf_op jit(solution)/shard_map/reduce_scatter | solution.py:216
  637.3 33.7 %reduce-scatter.9.cloned.1.call-done = bf16[256,1024]{0,1:T(8,128)(2,1)} async-done(((bf16[1024,1024]{0,1:T(8,128)(2,1)}), bf16[256,1024]{0,1:T(8,128)(2,1)}) %reduce-scatter.9.cloned.1.call-update) | async-done | bytes 524304 | tf_op jit(solution)/shard_map/reduce_scatter | solution.py:219
  680.8 9.9 fusion.60
  690.8 9.7 fusion.61
  701.6 9.7 fusion.41
  724.1 46.5 %all-reduce.4 = (f32[1024]{0:T(1024)S(1)}, f32[1024]{0:T(1024)S(1)}) all-reduce(f32[1024]{0:T(1024)S(1)} %get-tuple-element.116, f32[1024]{0:T(1024)S(1)} %get-tuple-element.114), channel_id=5, replica_groups=mesh['seq'=4,'batch'=8] {'seq','batch'}, use_global_device_ids=true, to_apply=%region_14.15.clone | all-reduce | flops 2048 | bytes 16384
  773.1 267.3 %reduce-scatter.11.cloned.1.call-done = f32[32,4096]{1,0:T(8,128)} async-done(((f32[1024,4096]{1,0:T(8,128)}), f32[32,4096]{1,0:T(8,128)}) %reduce-scatter.11.cloned.1.call-update) | async-done | bytes 524304 | tf_op jit(solution)/shard_map/reduce_scatter | solution.py:234
  1042.3 358.3 %reduce-scatter.13.cloned.1.call-done = f32[32,4096]{1,0:T(8,128)} async-done(((f32[1024,4096]{1,0:T(8,128)}), f32[32,4096]{1,0:T(8,128)}) %reduce-scatter.13.cloned.1.call-update) | async-done | bytes 524304 | tf_op jit(solution)/shard_map/reduce_scatter | solution.py:157
  1400.6 360.1 %reduce-scatter.15.cloned.1.call-done = f32[32,4096]{1,0:T(8,128)} async-done(((f32[1024,4096]{1,0:T(8,128)}), f32[32,4096]{1,0:T(8,128)}) %reduce-scatter.15.cloned.1.call-update) | async-done | bytes 524304 | tf_op jit(solution)/shard_map/reduce_scatter | solution.py:160
  1760.7 360.1 %reduce-scatter.17.cloned.1.call-done = f32[128,1024]{1,0:T(8,128)} async-done(((f32[4096,1024]{1,0:T(8,128)}), f32[128,1024]{1,0:T(8,128)}) %reduce-scatter.17.cloned.1.call-update) | async-done | bytes 524304 | tf_op jit(solution)/shard_map/reduce_scatter | solution.py:163
  (130 shorter events, 136.6 us)
Async XLA Ops:
  7.2 121.1 %copy-start.1 = (bf16[1,256,1024]{2,1,0:T(8,128)(2,1)S(1)}, bf16[1,256,1024]{2,1,0:T(8,128)(2,1)}, u32[]{:S(2)}) copy-start(bf16[1,256,1024]{2,1,0:T(8,128)(2,1)} %param.16) | copy-start | bytes 1572868
  7.2 62.9 %all-gather.10.cloned.1.call-start = ((), (), s32[]{:S(2)}) async-start(), calls=%async_computation.6 | async-start | bytes 2162688 | tf_op jit(solution)/shard_map/all_gather | solution.py:99
  7.9 120.4 %all-gather.16.cloned.1.call-start = ((), (), s32[]{:S(2)}) async-start(), calls=%async_computation.9 | async-start | bytes 2162688 | tf_op jit(solution)/shard_map/all_gather | solution.py:100
  8.7 177.9 %all-gather.14.cloned.1.call-start = ((), (), s32[]{:S(2)}) async-start(), calls=%async_computation.8 | async-start | bytes 2162688 | tf_op jit(solution)/shard_map/all_gather | solution.py:98
  9.4 200.6 %all-gather.12.cloned.1.call-start = ((), (), s32[]{:S(2)}) async-start(), calls=%async_computation.7 | async-start | bytes 2621440 | tf_op jit(solution)/shard_map/all_gather | solution.py:110
  73.4 161.1 %copy-start.18 = (s32[1,4]{1,0:T(1,128)S(1)}, s32[1,4]{1,0:T(1,128)}, u32[]{:S(2)}) copy-start(s32[1,4]{1,0:T(1,128)} %param.26) | copy-start | bytes 52
  73.5 161.1 %all-gather.18.cloned.1.call-start = ((), (), s32[]{:S(2)}) async-start(), calls=%async_computation.10 | async-start | bytes 2621440 | tf_op jit(solution)/shard_map/all_gather | solution.py:111
  131.5 162.3 %all-gather.20.cloned.1.call-start = ((), (), s32[]{:S(2)}) async-start(), calls=%async_computation.11 | async-start | bytes 2162688 | tf_op jit(solution)/shard_map/all_gather | solution.py:101
  132.1 240.7 %all-gather.22.cloned.1.call-start = ((), (), s32[]{:S(2)}) async-start(), calls=%async_computation.12 | async-start | bytes 8650752 | tf_op jit(solution)/shard_map/all_gather | solution.py:130
  132.8 318.6 %all-gather.24.cloned.1.call-start = ((), (), s32[]{:S(2)}) async-start(), calls=%async_computation.13 | async-start | bytes 8650752 | tf_op jit(solution)/shard_map/all_gather | solution.py:131
  133.6 396.6 %all-gather.26.cloned.1.call-start = ((), (), s32[]{:S(2)}) async-start(), calls=%async_computation.14 | async-start | bytes 8650752 | tf_op jit(solution)/shard_map/all_gather | solution.py:132
  134.3 503.0 %reduce-scatter.7.cloned.1.call-start = ((), (), s32[]{:S(2)}) async-start(), calls=%async_computation.15 | async-start | bytes 2621440 | tf_op jit(solution)/shard_map/reduce_scatter | solution.py:216
  251.2 45.0 %copy-start.5 = (bf16[256,1024]{0,1:T(8,128)(2,1)}, bf16[256,1024]{0,1:T(8,128)(2,1)S(1)}, u32[]{:S(2)}) copy-start(bf16[256,1024]{0,1:T(8,128)(2,1)S(1)} %get-tuple-element.143) | copy-start | bytes 1572868
  380.4 149.8 %copy-start.12 = (bf16[1,256,1024]{2,1,0:T(8,128)(2,1)S(1)}, bf16[1,256,1024]{2,1,0:T(8,128)(2,1)}, u32[]{:S(2)}) copy-start(bf16[1,256,1024]{2,1,0:T(8,128)(2,1)} %param.27) | copy-start | bytes 1572868
  574.9 13.4 copy-start.6
  588.3 15.4 slice-start
  594.8 8.9 slice-start.1
  594.8 8.9 copy-start.11
  607.3 63.7 %reduce-scatter.9.cloned.1.call-start = ((), (), s32[]{:S(2)}) async-start(), calls=%async_computation.16 | async-start | bytes 2621440 | tf_op jit(solution)/shard_map/reduce_scatter | solution.py:219
  608.1 432.3 %reduce-scatter.11.cloned.1.call-start = ((), (), s32[]{:S(2)}) async-start(), calls=%async_computation.17 | async-start | bytes 17301504 | tf_op jit(solution)/shard_map/reduce_scatter | solution.py:234
  680.6 720.0 %reduce-scatter.13.cloned.1.call-start = ((), (), s32[]{:S(2)}) async-start(), calls=%async_computation.18 | async-start | bytes 17301504 | tf_op jit(solution)/shard_map/reduce_scatter | solution.py:157
  690.8 1070.0 %reduce-scatter.15.cloned.1.call-start = ((), (), s32[]{:S(2)}) async-start(), calls=%async_computation.19 | async-start | bytes 17301504 | tf_op jit(solution)/shard_map/reduce_scatter | solution.py:160
  700.6 1420.3 %reduce-scatter.17.cloned.1.call-start = ((), (), s32[]{:S(2)}) async-start(), calls=%async_computation.20 | async-start | bytes 17301504 | tf_op jit(solution)/shard_map/reduce_scatter | solution.py:163
  721.2 50.5 %copy-start.17 = (f32[256]{0:T(256)S(1)}, f32[256]{0:T(256)}, u32[]{:S(2)}) copy-start(f32[256]{0:T(256)} %get-tuple-element.129) | copy-start | bytes 3076
  (13 other events, 60.5 us)
Sparse Core Ops, SparseCore 0:
  11.0 59.0 all-gather.9
  73.1 55.1 all-gather.15
  131.3 55.1 all-gather.13
  188.5 21.3 all-gather.11
  212.0 22.5 all-gather.17
  237.4 56.3 all-gather.19
  296.8 75.9 all-gather.21
  375.7 75.6 all-gather.23
  454.4 75.6 all-gather.25
  607.5 29.7 reduce-scatter.6
  639.8 31.1 reduce-scatter.8
  680.7 359.6 reduce-scatter.10
  1043.3 357.2 reduce-scatter.12
  1403.3 357.3 reduce-scatter.14
  1763.5 357.3 reduce-scatter.16
where the time goes:
time: 2130 us
  waiting for transfers between devices  1840 us (86%)
  matrix products  150 us (7%)
  blocking collectives  88.5 us (4%)
  local copies, waits for them, and re-layouts  24.9 us (1%)
    reduce_scatter x1, waiting for transfers between devices, local(): lax.psum_scatter(column_grad(normed_ffn, grad_up), ('seq', 'batch'), scat...  360 us
    reduce_scatter x1, waiting for transfers between devices, local(): lax.psum_scatter(column_grad(hidden, cot_rows), ('seq', 'batch'), scatter...  360 us
    reduce_scatter x1, waiting for transfers between devices, local(): lax.psum_scatter(column_grad(normed_ffn, grad_gate), ('seq', 'batch'), sc...  358 us
    reduce_scatter x1, waiting for transfers between devices, local(): lax.psum_scatter(jnp.concatenate([column_grad(normed_attn, projected_grad...  267 us
    unnamed x2, blocking collectives  88.5 us
    all_gather x1, waiting for transfers between devices, local(): lax.all_gather(w_gate, ('seq', 'batch'), axis=0, tiled=True)  76.3 us
    all_gather x1, waiting for transfers between devices, local(): lax.all_gather(w_up, ('seq', 'batch'), axis=0, tiled=True)  71 us
    all_gather x1, waiting for transfers between devices, local(): lax.all_gather(w_down, ('seq', 'batch'), axis=0, tiled=True)  71 us
  transfers between devices with their start and end apart: 15, of which 15 were waited for; matrix products, arithmetic and copies ran while one was open for 5% of the time, Pallas kernels for 0%

commit v1 on v0

--- a/solution.py
+++ b/solution.py
@@ -3,6 +3,7 @@
 import jax.numpy as jnp
 from jax import lax
 from jax.sharding import PartitionSpec as P
+from jax.lax import all_gather
 
 HEADS = 16
 EPSILON = 1e-05
@@ -107,8 +108,16 @@
     key_rows_mine = project(normed_attn, attn_full[1]).astype(jnp.bfloat16)
     value_rows_mine = project(normed_attn, attn_full[2]).astype(jnp.bfloat16)
     query_heads = split_heads(query)
-    key_block = lax.all_gather(key_rows_mine, "seq", axis=0, tiled=True)
-    value_block = lax.all_gather(value_rows_mine, "seq", axis=0, tiled=True)
+    key_block, value_block = jnp.split(
+        all_gather(
+            jnp.concatenate([key_rows_mine, value_rows_mine], axis=1),
+            axis_name="seq",
+            tiled=True,
+            axis=0,
+        ),
+        [key_rows_mine.shape[1]],
+        axis=1,
+    )
 
     def attend_compute(summed):
         gates, allowed = gating(query_heads, key_block)

time: 2130 us -> 2140 us (level)
    all_gather x1, waiting for transfers between devices: 15.1 us -> 55.7 us  [local(): lax.all_gather(w_key, ('seq', 'batch'), axis=0, tiled=True)]
    all_gather x1, waiting for transfers between devices: 54.8 us -> 15.1 us  [local(): lax.all_gather(w_value, ('seq', 'batch'), axis=0, tiled=True)]
    all_gather x2 -> x3, waiting for transfers between devices: 44.7 us -> 55.2 us  [the longest x1 31.7 us: local(): all_gather(jnp.concatenate([key_rows_mine, value_rows_mine], axis=1), axi...]
  transfers between devices with their start and end apart: 15 -> 16, of which waited for: 15 -> 15; matrix products, arithmetic and copies ran while one was open for 5% -> 6% of each run, Pallas kernels for 0% -> 0%
where the time goes in v1:
time: 2140 us
  waiting for transfers between devices  1850 us (86%)
  matrix products  149 us (7%)
  blocking collectives  87.2 us (4%)
  local copies, waits for them, and re-layouts  29.3 us (1%)
    reduce_scatter x1, waiting for transfers between devices, local(): lax.psum_scatter(column_grad(hidden, cot_rows), ('seq', 'batch'), scatter...  360 us
    reduce_scatter x1, waiting for transfers between devices, local(): lax.psum_scatter(column_grad(normed_ffn, grad_up), ('seq', 'batch'), scat...  360 us
    reduce_scatter x1, waiting for transfers between devices, local(): lax.psum_scatter(column_grad(normed_ffn, grad_gate), ('seq', 'batch'), sc...  358 us
    reduce_scatter x1, waiting for transfers between devices, local(): lax.psum_scatter(jnp.concatenate([column_grad(normed_attn, projected_grad...  269 us
    unnamed x2, blocking collectives  87.2 us
    all_gather x1, waiting for transfers between devices, local(): lax.all_gather(w_gate, ('seq', 'batch'), axis=0, tiled=True)  76.2 us
    all_gather x1, waiting for transfers between devices, local(): lax.all_gather(w_up, ('seq', 'batch'), axis=0, tiled=True)  71 us
    all_gather x1, waiting for transfers between devices, local(): lax.all_gather(w_down, ('seq', 'batch'), axis=0, tiled=True)  71 us
  transfers between devices with their start and end apart: 16, of which 15 were waited for; matrix products, arithmetic and copies ran while one was open for 6% of the time, Pallas kernels for 0%

profile of v1, /device:TPU:0, one launch (start us, length us, event | category | flops | bytes accessed | tf_op | source)
XLA Modules:
  0.0 2139.5 jit_solution(7476101424045387695)
XLA Ops:
  11.2 42.1 %all-reduce.5 = (bf16[1024]{0:T(1024)(128)(2,1)S(1)}, bf16[1024]{0:T(1024)(128)(2,1)S(1)}) all-reduce(bf16[1024]{0:T(1024)(128)(2,1)S(1)} %dynamic-update-slice, bf16[1024]{0:T(1024)(128)(2,1)S(1)} %dynamic-update-slice.1), channel_id=1, replica_groups=mesh['seq'=4,'batch'=8] {'seq','batch'}, use_global_device_ids=true, to_apply=%add | all-reduce | flops 2048 | bytes 8192
  55.0 15.1 all-gather.13.cloned.1.call-done
  72.6 55.7 %all-gather.11.cloned.1.call-done = bf16[1024,1024]{1,0:T(8,128)(2,1)} async-done(((bf16[32,1024]{1,0:T(8,128)(2,1)}), bf16[1024,1024]{1,0:T(8,128)(2,1)}) %all-gather.11.cloned.1.call-update) | async-done | bytes 2097168 | tf_op jit(solution)/shard_map/all_gather | solution.py:100
  135.3 51.2 %all-gather.17.cloned.1.call-done = bf16[1024,1024]{1,0:T(8,128)(2,1)} async-done(((bf16[32,1024]{1,0:T(8,128)(2,1)}), bf16[1024,1024]{1,0:T(8,128)(2,1)}) %all-gather.17.cloned.1.call-update) | async-done | bytes 2097168 | tf_op jit(solution)/shard_map/all_gather | solution.py:99
  190.1 31.7 %all-gather.15.cloned.1.call-done = bf16[1024,2048]{1,0:T(8,128)(2,1)} async-done(((bf16[256,2048]{1,0:T(8,128)(2,1)}), bf16[1024,2048]{1,0:T(8,128)(2,1)}) %all-gather.15.cloned.1.call-update) | async-done | bytes 4194320 | tf_op jit(solution)/shard_map/all_gather | solution.py:112
  221.9 21.1 conditional.2
  242.9 38.2 %all-gather.19.cloned.1.call-done = bf16[1024,1024]{1,0:T(8,128)(2,1)} async-done(((bf16[32,1024]{1,0:T(8,128)(2,1)}), bf16[1024,1024]{1,0:T(8,128)(2,1)}) %all-gather.19.cloned.1.call-update) | async-done | bytes 2097168 | tf_op jit(solution)/shard_map/all_gather | solution.py:102
  283.7 76.2 %all-gather.21.cloned.1.call-done = bf16[1024,4096]{1,0:T(8,128)(2,1)} async-done(((bf16[32,4096]{1,0:T(8,128)(2,1)}), bf16[1024,4096]{1,0:T(8,128)(2,1)}) %all-gather.21.cloned.1.call-update) | async-done | bytes 8388624 | tf_op jit(solution)/shard_map/all_gather | solution.py:139
  367.6 71.0 %all-gather.23.cloned.1.call-done = bf16[1024,4096]{1,0:T(8,128)(2,1)} async-done(((bf16[32,4096]{1,0:T(8,128)(2,1)}), bf16[1024,4096]{1,0:T(8,128)(2,1)}) %all-gather.23.cloned.1.call-update) | async-done | bytes 8388624 | tf_op jit(solution)/shard_map/all_gather | solution.py:140
  446.4 71.0 %all-gather.25.cloned.1.call-done = bf16[4096,1024]{1,0:T(8,128)(2,1)} async-done(((bf16[128,1024]{1,0:T(8,128)(2,1)}), bf16[4096,1024]{1,0:T(8,128)(2,1)}) %all-gather.25.cloned.1.call-update) | async-done | bytes 8388624 | tf_op jit(solution)/shard_map/all_gather | solution.py:141
  517.3 12.5 multiply_convert_fusion
  541.8 23.5 %all-gather.29.cloned.1.call-done = bf16[1024,1024]{1,0:T(8,128)(2,1)} async-done(((bf16[256,1024]{1,0:T(8,128)(2,1)}), bf16[1024,1024]{1,0:T(8,128)(2,1)}) %all-gather.29.cloned.1.call-update) | async-done | bytes 2097168 | tf_op jit(solution)/shard_map/all_gather | solution.py:190
  565.3 52.8 %conditional.3 = (bf16[1024,1024]{0,1:T(8,128)(2,1)}, bf16[1024,1024]{0,1:T(8,128)(2,1)}, bf16[256,1024]{0,1:T(8,128)(2,1)}) conditional(s32[]{:T(128)} %convert_element_type.97, () %tuple.28, (s32[4]{0:T(128)S(1)}, s32[1,4]{1,0:T(1,128)S(1)}, s32[256]{0:T(256)S(1)}, bf16[256,1024]{1,0:T(8,128)(2,1)}, bf16[1024,1024]{1,0:T(8,128)(2,1)}, ...), branch_computations={%region_6.7_spmd, %region_7.9_spmd} | conditional | flops 2733668352 | bytes 134499488 | solution.py:221
  585.6 13.4 select_convert_fusion.2
  622.5 27.0 %reduce-scatter.7.cloned.1.call-done = bf16[256,1024]{0,1:T(8,128)(2,1)} async-done(((bf16[1024,1024]{0,1:T(8,128)(2,1)}), bf16[256,1024]{0,1:T(8,128)(2,1)}) %reduce-scatter.7.cloned.1.call-update) | async-done | bytes 524304 | tf_op jit(solution)/shard_map/reduce_scatter | solution.py:225
  649.5 33.6 %reduce-scatter.9.cloned.1.call-done = bf16[256,1024]{0,1:T(8,128)(2,1)} async-done(((bf16[1024,1024]{0,1:T(8,128)(2,1)}), bf16[256,1024]{0,1:T(8,128)(2,1)}) %reduce-scatter.9.cloned.1.call-update) | async-done | bytes 524304 | tf_op jit(solution)/shard_map/reduce_scatter | solution.py:228
  692.9 9.9 fusion.61
  702.9 9.7 fusion.62
  713.7 9.7 fusion.41
  736.2 45.2 %all-reduce.4 = (f32[1024]{0:T(1024)S(1)}, f32[1024]{0:T(1024)S(1)}) all-reduce(f32[1024]{0:T(1024)S(1)} %get-tuple-element.112, f32[1024]{0:T(1024)S(1)} %get-tuple-element.110), channel_id=5, replica_groups=mesh['seq'=4,'batch'=8] {'seq','batch'}, use_global_device_ids=true, to_apply=%region_14.15.clone | all-reduce | flops 2048 | bytes 16384
  783.8 268.6 %reduce-scatter.11.cloned.1.call-done = f32[32,4096]{1,0:T(8,128)} async-done(((f32[1024,4096]{1,0:T(8,128)}), f32[32,4096]{1,0:T(8,128)}) %reduce-scatter.11.cloned.1.call-update) | async-done | bytes 524304 | tf_op jit(solution)/shard_map/reduce_scatter | solution.py:243
  1054.4 358.2 %reduce-scatter.13.cloned.1.call-done = f32[32,4096]{1,0:T(8,128)} async-done(((f32[1024,4096]{1,0:T(8,128)}), f32[32,4096]{1,0:T(8,128)}) %reduce-scatter.13.cloned.1.call-update) | async-done | bytes 524304 | tf_op jit(solution)/shard_map/reduce_scatter | solution.py:166
  1412.6 360.1 %reduce-scatter.15.cloned.1.call-done = f32[32,4096]{1,0:T(8,128)} async-done(((f32[1024,4096]{1,0:T(8,128)}), f32[32,4096]{1,0:T(8,128)}) %reduce-scatter.15.cloned.1.call-update) | async-done | bytes 524304 | tf_op jit(solution)/shard_map/reduce_scatter | solution.py:169
  1772.7 360.1 %reduce-scatter.17.cloned.1.call-done = f32[128,1024]{1,0:T(8,128)} async-done(((f32[4096,1024]{1,0:T(8,128)}), f32[128,1024]{1,0:T(8,128)}) %reduce-scatter.17.cloned.1.call-update) | async-done | bytes 524304 | tf_op jit(solution)/shard_map/reduce_scatter | solution.py:172
  (134 shorter events, 141.4 us)
Async XLA Ops:
  7.2 121.1 %copy-start.1 = (bf16[1,256,1024]{2,1,0:T(8,128)(2,1)S(1)}, bf16[1,256,1024]{2,1,0:T(8,128)(2,1)}, u32[]{:S(2)}) copy-start(bf16[1,256,1024]{2,1,0:T(8,128)(2,1)} %param.16) | copy-start | bytes 1572868
  7.2 62.9 %all-gather.13.cloned.1.call-start = ((), (), s32[]{:S(2)}) async-start(), calls=%async_computation.7 | async-start | bytes 2162688 | tf_op jit(solution)/shard_map/all_gather | solution.py:101
  7.9 120.4 %all-gather.11.cloned.1.call-start = ((), (), s32[]{:S(2)}) async-start(), calls=%async_computation.6 | async-start | bytes 2162688 | tf_op jit(solution)/shard_map/all_gather | solution.py:100
  8.7 177.9 %all-gather.17.cloned.1.call-start = ((), (), s32[]{:S(2)}) async-start(), calls=%async_computation.9 | async-start | bytes 2162688 | tf_op jit(solution)/shard_map/all_gather | solution.py:99
  9.4 212.5 %all-gather.15.cloned.1.call-start = ((), (), s32[]{:S(2)}) async-start(), calls=%async_computation.8 | async-start | bytes 5242880 | tf_op jit(solution)/shard_map/all_gather | solution.py:112
  72.6 61.9 %copy-start.13 = (bf16[256,1024]{1,0:T(8,128)(2,1)}, bf16[256,1024]{1,0:T(8,128)(2,1)S(1)}, u32[]{:S(2)}) copy-start(bf16[256,1024]{1,0:T(8,128)(2,1)S(1)} %convolution_convert_fusion.2) | copy-start | bytes 1572868
  130.7 59.2 %copy-start.14 = (bf16[256,1024]{1,0:T(8,128)(2,1)}, bf16[256,1024]{1,0:T(8,128)(2,1)S(1)}, u32[]{:S(2)}) copy-start(bf16[256,1024]{1,0:T(8,128)(2,1)S(1)} %convolution_convert_fusion.3) | copy-start | bytes 1572868
  131.8 90.1 %copy-start.18 = (s32[1,4]{1,0:T(1,128)S(1)}, s32[1,4]{1,0:T(1,128)}, u32[]{:S(2)}) copy-start(s32[1,4]{1,0:T(1,128)} %param.26) | copy-start | bytes 52
  131.8 149.3 %all-gather.19.cloned.1.call-start = ((), (), s32[]{:S(2)}) async-start(), calls=%async_computation.10 | async-start | bytes 2162688 | tf_op jit(solution)/shard_map/all_gather | solution.py:102
  132.4 227.5 %all-gather.21.cloned.1.call-start = ((), (), s32[]{:S(2)}) async-start(), calls=%async_computation.11 | async-start | bytes 8650752 | tf_op jit(solution)/shard_map/all_gather | solution.py:139
  133.0 305.6 %all-gather.23.cloned.1.call-start = ((), (), s32[]{:S(2)}) async-start(), calls=%async_computation.12 | async-start | bytes 8650752 | tf_op jit(solution)/shard_map/all_gather | solution.py:140
  133.8 383.6 %all-gather.25.cloned.1.call-start = ((), (), s32[]{:S(2)}) async-start(), calls=%async_computation.13 | async-start | bytes 8650752 | tf_op jit(solution)/shard_map/all_gather | solution.py:141
  134.5 407.3 %all-gather.27.cloned.1.call-start = ((), (), s32[]{:S(2)}) async-start(), calls=%async_computation.14 | async-start | bytes 2621440 | tf_op jit(solution)/shard_map/all_gather | solution.py:191
  135.2 430.0 %all-gather.29.cloned.1.call-start = ((), (), s32[]{:S(2)}) async-start(), calls=%async_computation.15 | async-start | bytes 2621440 | tf_op jit(solution)/shard_map/all_gather | solution.py:190
  189.9 459.6 %reduce-scatter.7.cloned.1.call-start = ((), (), s32[]{:S(2)}) async-start(), calls=%async_computation.16 | async-start | bytes 2621440 | tf_op jit(solution)/shard_map/reduce_scatter | solution.py:225
  242.9 124.7 %copy-start.4 = (bf16[256,1024]{0,1:T(8,128)(2,1)}, bf16[256,1024]{0,1:T(8,128)(2,1)S(1)}, u32[]{:S(2)}) copy-start(bf16[256,1024]{0,1:T(8,128)(2,1)S(1)} %get-tuple-element.141) | copy-start | bytes 1572868
  367.6 149.8 %copy-start.10 = (bf16[1,256,1024]{2,1,0:T(8,128)(2,1)S(1)}, bf16[1,256,1024]{2,1,0:T(8,128)(2,1)}, u32[]{:S(2)}) copy-start(bf16[1,256,1024]{2,1,0:T(8,128)(2,1)} %param.27) | copy-start | bytes 1572868
  598.9 15.6 slice-start
  618.1 64.9 %reduce-scatter.9.cloned.1.call-start = ((), (), s32[]{:S(2)}) async-start(), calls=%async_computation.17 | async-start | bytes 2621440 | tf_op jit(solution)/shard_map/reduce_scatter | solution.py:228
  618.7 433.8 %reduce-scatter.11.cloned.1.call-start = ((), (), s32[]{:S(2)}) async-start(), calls=%async_computation.18 | async-start | bytes 17301504 | tf_op jit(solution)/shard_map/reduce_scatter | solution.py:243
  692.7 719.9 %reduce-scatter.13.cloned.1.call-start = ((), (), s32[]{:S(2)}) async-start(), calls=%async_computation.19 | async-start | bytes 17301504 | tf_op jit(solution)/shard_map/reduce_scatter | solution.py:166
  702.9 1069.8 %reduce-scatter.15.cloned.1.call-start = ((), (), s32[]{:S(2)}) async-start(), calls=%async_computation.20 | async-start | bytes 17301504 | tf_op jit(solution)/shard_map/reduce_scatter | solution.py:169
  712.7 1420.1 %reduce-scatter.17.cloned.1.call-start = ((), (), s32[]{:S(2)}) async-start(), calls=%async_computation.21 | async-start | bytes 17301504 | tf_op jit(solution)/shard_map/reduce_scatter | solution.py:172
  733.3 49.2 %copy-start.17 = (f32[256]{0:T(256)S(1)}, f32[256]{0:T(256)}, u32[]{:S(2)}) copy-start(f32[256]{0:T(256)} %get-tuple-element.127) | copy-start | bytes 3076
  (14 other events, 74.5 us)
Sparse Core Ops, SparseCore 0:
  11.0 59.0 all-gather.12
  73.1 55.2 all-gather.10
  131.3 55.2 all-gather.16
  188.5 33.2 all-gather.14
  224.7 56.3 all-gather.18
  283.9 75.9 all-gather.20
  362.9 75.6 all-gather.22
  441.6 75.6 all-gather.24
  519.5 21.1 all-gather.26
  542.7 22.5 all-gather.28
  618.3 31.1 reduce-scatter.6
  651.9 31.1 reduce-scatter.8
  692.8 359.6 reduce-scatter.10
  1055.2 357.3 reduce-scatter.12
  1415.3 357.3 reduce-scatter.14
  1775.4 357.3 reduce-scatter.16
